TPU v7x, 32 devices: a whole 2x2x4 slice. The times are simulated.
32 devices in a mesh: mem: 8 (over z, x), feat: 4 (over y, core).
Axes of the slice: x: 2, y: 2, z: 4, core: 2. Of those that a mesh axis runs over, the one named last changes fastest.
Arguments:
- events: bfloat16 [2048, 32, 256], P('mem'), may hold values from -6 to 6
- w_in: bfloat16 [256, 1024], P(None, 'feat'), may hold values from -0.375 to 0.375
- w_out: bfloat16 [1024, 256], P('feat'), may hold values from -0.1875 to 0.1875
- probe_vectors: bfloat16 [2048, 256], P(('mem', 'feat')), may hold values from -8 to 8
- key_queue: bfloat16 [65536, 256], P('mem'), may hold values from -1 to 1
- target_position: int32 [2048], P(('mem', 'feat')), may hold values from 0 to 65535
- pointer: int32 [1], replicated, may hold values from 0 to 65535
Outputs:
- loss: float32 [2048], P(('mem', 'feat'))
- probe_derivative: float32 [2048, 256], P(('mem', 'feat'))
- new_memory: bfloat16 [65536, 256], P('mem')
All inputs are finite; a program needn't handle non-finite values.
Results may differ from a plain program's by a relative error of at most 0.0017.
Values may be sent and summed in bfloat16 or wider, within the bound.
A program may use at most 64 MiB of HBM per device.

v0:
```python
import functools

import jax
import jax.numpy as jnp
from jax import lax
from jax.experimental import pallas as pl
from jax.experimental.pallas import tpu as pltpu
from jax.sharding import PartitionSpec as P

inverse_softness = 14.0
epsilon = 1e-06
log2e = 1.4426950408889634
MESH = pl.DeviceIdType.MESH
ANY = pl.BlockSpec(memory_space=pl.ANY)
VMEM = pl.BlockSpec(memory_space=pltpu.VMEM)
HBM = pl.BlockSpec(memory_space=pltpu.HBM)


def step_kernel(
    n, nf, ev_chunk, slot_block, q_chunk,
    ev_hbm, w_in_ref, w_out_ref, probe_ref, queue_hbm, target_ref,
    loss_ref, grad_ref, keys_ref,
    ev, queue, q_all, t_all, pooled, partial, part_in, pos, m_s, l_s, acc,
    pair_out, pair_in, stat_out, stat_in, gout, g_in,
    ev_sem, queue_sem, q_ss, q_rs, t_ss, t_rs, p_ss, p_rs, k_ss, k_rs, y_ss, y_rs, c_ss, c_rs,
    s_ss, s_rs, g_ss, g_rs, h_ss, h_rs,
):
    me = lax.axis_index("mem")
    mf = lax.axis_index("feat")
    own = probe_ref.shape[0]
    rows_q = q_all.shape[0]
    slots, width = queue.shape
    ev_rows = ev.shape[0]
    n_ev, n_blk = ev_rows // ev_chunk, slots // slot_block
    sessions = pooled.shape[0]
    part_rows = sessions // nf

    def ev_copy(i):
        span = pl.ds(pl.multiple_of(i * ev_chunk, ev_chunk), ev_chunk)
        return pltpu.make_async_copy(ev_hbm.at[span], ev.at[span], ev_sem.at[i])

    def queue_copy(i):
        span = pl.ds(pl.multiple_of(i * slot_block, slot_block), slot_block)
        return pltpu.make_async_copy(queue_hbm.at[span], queue.at[span], queue_sem.at[i])

    partner = me + 1 - 2 * lax.rem(me, 2)

    def mem_peer(k):
        return (lax.rem(me + k, n), mf)

    def feat_peer(k):
        return (me, lax.rem(mf + k, nf))

    def block_id(i):
        return lax.rem(me + n - i, n) if i % 2 == 0 else lax.rem(partner + n - (i - 1), n)

    barrier = pltpu.get_barrier_semaphore()
    for k in range(1, n):
        pl.semaphore_signal(barrier, inc=1, device_id=mem_peer(k), device_id_type=MESH)
    for k in range(1, nf):
        pl.semaphore_signal(barrier, inc=1, device_id=feat_peer(k), device_id_type=MESH)
    for i in range(n_ev):
        ev_copy(i).start()
    for i in range(n_blk):
        queue_copy(i).start()

    def own_span(m):
        return pl.ds(pl.multiple_of(m * own, own), own)

    q_all[own_span(me), :] = probe_ref[...]
    t_all[me] = target_ref[...]
    pl.semaphore_wait(barrier, n - 1 + nf - 1)

    def remote(src, dst, ss, rs, to):
        return pltpu.make_async_remote_copy(
            src_ref=src, dst_ref=dst, send_sem=ss, recv_sem=rs, device_id=to, device_id_type=MESH
        )

    t_copies = [
        remote(target_ref, t_all.at[me], t_ss.at[k], t_rs.at[k], mem_peer(k)) for k in range(1, n)
    ]
    q_copies = {
        k: remote(probe_ref, q_all.at[own_span(me)], q_ss.at[k], q_rs.at[k], mem_peer(k))
        for k in range(2, n, 2)
    }
    q_copies[1] = remote(
        probe_ref, q_all.at[own_span(me)], q_ss.at[1], q_rs.at[1], (partner, mf)
    )
    for a in q_copies.values():
        a.start()
    for a in t_copies:
        a.start()

    events_of = ev_rows // sessions
    c1 = 0.7978845608028654
    c2 = c1 * 0.044715

    def encode(i, carry):
        ev_copy(i).wait()
        rows = ev[pl.ds(pl.multiple_of(i * ev_chunk, ev_chunk), ev_chunk), :]
        x = jnp.dot(rows, w_in_ref[...], preferred_element_type=jnp.float32)
        t = jnp.tanh(x * (c1 + c2 * (x * x)))
        y = x * t + x
        y = y.reshape(ev_chunk // events_of, events_of, y.shape[1])
        mean = jnp.sum(y, axis=1) * (0.5 / events_of)
        s = ev_chunk // events_of
        pooled[pl.ds(pl.multiple_of(i * s, s), s), :] = mean.astype(jnp.bfloat16)
        return carry

    lax.fori_loop(0, n_ev, encode, 0)
    partial[...] = jnp.dot(pooled[...], w_out_ref[...], preferred_element_type=jnp.float32)

    def part_span(f):
        return pl.ds(pl.multiple_of(f * part_rows, part_rows), part_rows)

    p_copies = []
    for k in range(1, nf):
        to = feat_peer(k)
        p_copies.append(
            remote(partial.at[part_span(to[1])], part_in.at[k], p_ss.at[k], p_rs.at[k], to)
        )
        p_copies[-1].start()

    for k in range(2, n, 2):
        q_copies[k].wait_recv()
        span = own_span(block_id(k))
        q_copies[k + 1] = remote(
            q_all.at[span], q_all.at[span], q_ss.at[k + 1], q_rs.at[k + 1], (partner, mf)
        )
        q_copies[k + 1].start()
    for a in t_copies:
        a.wait()

    diag = lax.broadcasted_iota(jnp.int32, (own, own), 0) == lax.broadcasted_iota(
        jnp.int32, (own, own), 1
    )

    def as_column(row):
        wide = jnp.broadcast_to(row, (own, own))
        return jnp.sum(jnp.where(diag, wide, 0.0), axis=1, keepdims=True)

    for j in range(n):
        local = as_column(t_all[j].astype(jnp.float32)).astype(jnp.int32) - me * slots
        pos[j * own : (j + 1) * own, :] = jnp.broadcast_to(local, (own, 128))

    acc[...] = jnp.zeros(acc.shape, jnp.float32)

    def pick(b, carry):
        queue_copy(b).wait()
        kb = queue[pl.ds(pl.multiple_of(b * slot_block, slot_block), slot_block), :]
        for c in range(rows_q // q_chunk):
            rs = slice(c * q_chunk, (c + 1) * q_chunk)
            at = lax.broadcasted_iota(jnp.int32, (q_chunk, slot_block), 1)
            hit = at == (pos[rs, :1] - b * slot_block)
            acc[rs, :] += jnp.dot(
                jnp.where(hit, 1.0, 0.0).astype(jnp.bfloat16), kb, preferred_element_type=jnp.float32
            )
        return carry

    lax.fori_loop(0, n_blk, pick, 0)
    pair_out[...] = acc[...].astype(jnp.bfloat16)
    h_copies = []
    for k in range(1, n):
        to = mem_peer(k)
        h_copies.append(
            remote(pair_out.at[own_span(to[0])], pair_in.at[k], h_ss.at[k], h_rs.at[k], to)
        )
        h_copies[-1].start()

    for k in range(1, n, 2):
        q_copies[k].wait_recv()

    m_s[...] = jnp.full(m_s.shape, -jnp.inf, jnp.float32)
    l_s[...] = jnp.zeros(l_s.shape, jnp.float32)
    acc[...] = jnp.zeros(acc.shape, jnp.float32)
    scale2 = inverse_softness * log2e

    def attend(b, carry):
        kb = queue[pl.ds(pl.multiple_of(b * slot_block, slot_block), slot_block), :]
        for c in range(rows_q // q_chunk):
            rs = slice(c * q_chunk, (c + 1) * q_chunk)
            s = lax.dot_general(
                q_all[rs, :], kb, (((1,), (1,)), ((), ())), preferred_element_type=jnp.float32
            )
            m_old = m_s[rs, :1]
            m_new = jnp.maximum(m_old, jnp.max(s, axis=1, keepdims=True))
            p = jnp.exp2((s - m_new) * scale2)
            alpha = jnp.exp2((m_old - m_new) * scale2)
            m_s[rs, :] = jnp.broadcast_to(m_new, (q_chunk, 128))
            l_new = l_s[rs, :1] * alpha + jnp.sum(p, axis=1, keepdims=True)
            l_s[rs, :] = jnp.broadcast_to(l_new, (q_chunk, 128))
            acc[rs, :] = acc[rs, :] * alpha + jnp.dot(
                p.astype(jnp.bfloat16), kb, preferred_element_type=jnp.float32
            )
        return carry

    stage_a, stage_b = n_blk // 8, (5 * n_blk) // 8
    lax.fori_loop(0, stage_a, attend, 0)

    for a in p_copies:
        a.wait()
    raw = partial[part_span(mf), :]
    for k in range(1, nf):
        raw = raw + part_in[k]
    scaled = raw * lax.rsqrt(jnp.mean(raw * raw, axis=1, keepdims=True) + epsilon) / 16.0

    def key_span(m, f):
        return pl.ds(pl.multiple_of((m * nf + f) * part_rows, part_rows), part_rows)

    mine = key_span(me, mf)
    keys_ref[mine, :] = scaled.astype(jnp.bfloat16)
    far_feat = lax.rem(mf + nf // 2, nf)
    far = (me, far_feat)
    near = (me, mf + 1 - 2 * lax.rem(mf, 2))

    def to_same(span, ss, rs, i, to):
        a = remote(keys_ref.at[span], keys_ref.at[span], ss.at[i], rs.at[i], to)
        a.start()
        return a

    k_copies = {k: to_same(mine, k_ss, k_rs, k, mem_peer(k)) for k in range(2, n, 2)}
    k_copies[1] = to_same(mine, k_ss, k_rs, 1, (partner, mf))
    y_copies = {0: to_same(mine, y_ss, y_rs, 0, far)}
    c_copies = {0: to_same(mine, c_ss, c_rs, 0, near)}

    lax.fori_loop(stage_a, stage_b, attend, 0)

    for k in range(2, n, 2):
        k_copies[k].wait_recv()
        span = key_span(block_id(k), mf)
        k_copies[k + 1] = to_same(span, k_ss, k_rs, k + 1, (partner, mf))
        y_copies[k] = to_same(span, y_ss, y_rs, k, far)
        c_copies[k] = to_same(span, c_ss, c_rs, k, near)

    lax.fori_loop(stage_b, n_blk, attend, 0)

    gout[...] = acc[...].astype(jnp.bfloat16)
    g_copies = []
    for k in range(1, n):
        to = mem_peer(k)
        g_copies.append(remote(gout.at[own_span(to[0])], g_in.at[k], g_ss.at[k], g_rs.at[k], to))
        g_copies[-1].start()
    lane = lax.broadcasted_iota(jnp.int32, m_s.shape, 1)
    packed = jnp.where(lane == 0, m_s[...], l_s[...]).T
    for j in range(n):
        stat_out[j, 0:2, :] = packed[0:2, j * own : (j + 1) * own]
    s_copies = []
    for k in range(1, n):
        to = mem_peer(k)
        s_copies.append(remote(stat_out.at[to[0]], stat_in.at[k], s_ss.at[k], s_rs.at[k], to))
        s_copies[-1].start()

    for i in range(1, n, 2):
        k_copies[i].wait_recv()
        span = key_span(block_id(i), mf)
        y_copies[i] = to_same(span, y_ss, y_rs, i, far)
        c_copies[i] = to_same(span, c_ss, c_rs, i, near)

    paired = pair_out[own_span(me), :].astype(jnp.float32)
    for a in h_copies:
        a.wait()
    for k in range(1, n):
        paired = paired + pair_in[k].astype(jnp.float32)
    score = jnp.sum(probe_ref[...].astype(jnp.float32) * paired, axis=1, keepdims=True)
    score = jnp.sum(
        jnp.where(diag, jnp.broadcast_to(score, (own, own)), 0.0), axis=0, keepdims=True
    )

    order = [0] + list(range(2, n, 2)) + list(range(1, n, 2))
    for i in order:
        y_copies[i].wait_recv()
        c_copies[n + i] = to_same(key_span(block_id(i), far_feat), c_ss, c_rs, n + i, near)

    for a in s_copies:
        a.wait()
    stats = [stat_out[me]] + [stat_in[k] for k in range(1, n)]
    top = stats[0][0:1, :]
    for st in stats[1:]:
        top = jnp.maximum(top, st[0:1, :])
    powers = [jnp.exp2((st[0:1, :] - top) * scale2) for st in stats]
    total = stats[0][1:2, :] * powers[0]
    for st, w in zip(stats[1:], powers[1:]):
        total = total + st[1:2, :] * w
    loss_ref[...] = (top - score) * inverse_softness + jnp.log(total)
    grad = acc[own_span(me), :] * as_column(powers[0] / total)
    for k in range(1, n):
        g_copies[k - 1].wait()
        grad = grad + g_in[k].astype(jnp.float32) * as_column(powers[k] / total)
    grad_ref[...] = inverse_softness * (grad - paired)

    for a in list(q_copies.values()) + list(k_copies.values()) + list(y_copies.values()):
        a.wait_send()
    for a in c_copies.values():
        a.wait()


def fill_kernel(
    block, start_ref, keys_hbm, queue_ref, loss_in, grad_in,
    loss_ref, grad_ref, out_hbm,
    keys, rolled, merged, keys_sem, out_sem,
):
    start = start_ref[0]
    count = keys.shape[0]
    slots, width = queue_ref.shape
    phase = jnp.bitwise_and(start, 15)
    blocks = slots // block
    here = (start < slots) & (start + count > 0)
    keys_copy = pltpu.make_async_copy(keys_hbm, keys, keys_sem)

    @pl.when(here)
    def _():
        keys_copy.start()

    def spans(i):
        return slice(i * block, (i + 1) * block)

    def inside(i):
        return (i * block < start + count) & ((i + 1) * block > start)

    def plain(i):
        return pltpu.make_async_copy(queue_ref.at[spans(i)], out_hbm.at[spans(i)], out_sem.at[i])

    for i in range(blocks):

        @pl.when(jnp.logical_not(inside(i)))
        def _():
            plain(i).start()

    loss_ref[...] = loss_in[...]
    grad_ref[...] = grad_in[...]

    @pl.when(here)
    def _():
        keys_copy.wait()
        tile = min(256, count)
        for c in range(count // tile + 1):
            lo = max(c * tile - 16, 0)
            hi = min(c * tile + tile, count)
            x = keys[lo:hi, :].astype(jnp.float32)
            if c == 0:
                x = jnp.concatenate([jnp.zeros((16, width), jnp.float32), x], axis=0)
            if c == count // tile:
                x = jnp.concatenate([x, jnp.zeros((16, width), jnp.float32)], axis=0)
            x = pltpu.roll(x, phase, 0)[16:, :]
            at = block + c * tile
            rolled[at : at + x.shape[0], :] = x.astype(jnp.bfloat16)

    for i in range(blocks):

        @pl.when(inside(i))
        def _():
            at = pl.multiple_of(block + i * block - (start - phase), 16)
            row = lax.broadcasted_iota(jnp.int32, (block, width), 0) + (i * block - start)
            take = (row >= 0) & (row < count)
            new = rolled[pl.ds(at, block), :].astype(jnp.float32)
            old = queue_ref[spans(i), :].astype(jnp.float32)
            merged[spans(i), :] = jnp.where(take, new, old).astype(jnp.bfloat16)
            pltpu.make_async_copy(
                merged.at[spans(i)], out_hbm.at[spans(i)], out_sem.at[i]
            ).start()

    for i in range(blocks):
        plain(i).wait()


def shards(events, w_in, w_out, probe_vectors, key_queue, target_position, pointer):
    n, nf = lax.axis_size("mem"), lax.axis_size("feat")
    sessions, per, depth = events.shape
    own, width = probe_vectors.shape
    slots = key_queue.shape[0]
    rows_q = own * n
    hidden = w_in.shape[1]
    flat = events.reshape(sessions * per, depth)
    ev_chunk = min(1024, flat.shape[0])
    slot_block = min(1024, slots)
    q_chunk = min(256, rows_q)
    part_rows = sessions // nf
    f32, bf16 = jnp.float32, jnp.bfloat16
    dma = pltpu.SemaphoreType.DMA
    loss, grad, keys = pl.pallas_call(
        functools.partial(step_kernel, n, nf, ev_chunk, slot_block, q_chunk),
        out_shape=(
            jax.ShapeDtypeStruct((1, own), f32),
            jax.ShapeDtypeStruct((own, width), f32),
            jax.ShapeDtypeStruct((sessions * n, width), bf16),
        ),
        in_specs=[ANY, VMEM, VMEM, VMEM, ANY, VMEM],
        out_specs=(VMEM, VMEM, VMEM),
        scratch_shapes=[
            pltpu.VMEM(flat.shape, bf16),
            pltpu.VMEM(key_queue.shape, bf16),
            pltpu.VMEM((rows_q, width), bf16),
            pltpu.VMEM((n, 1, own), jnp.int32),
            pltpu.VMEM((sessions, hidden), bf16),
            pltpu.VMEM((sessions, width), f32),
            pltpu.VMEM((nf, part_rows, width), f32),
            pltpu.VMEM((rows_q, 128), jnp.int32),
            pltpu.VMEM((rows_q, 128), f32),
            pltpu.VMEM((rows_q, 128), f32),
            pltpu.VMEM((rows_q, width), f32),
            pltpu.VMEM((rows_q, width), bf16),
            pltpu.VMEM((n, own, width), bf16),
            pltpu.VMEM((n, 4, own), f32),
            pltpu.VMEM((n, 4, own), f32),
            pltpu.VMEM((rows_q, width), bf16),
            pltpu.VMEM((n, own, width), bf16),
            dma((flat.shape[0] // ev_chunk,)),
            dma((slots // slot_block,)),
            dma((n,)), dma((n,)), dma((n,)), dma((n,)),
            dma((nf,)), dma((nf,)),
            dma((n,)), dma((n,)),
            dma((n,)), dma((n,)),
            dma((2 * n,)), dma((2 * n,)),
            dma((n,)), dma((n,)),
            dma((n,)), dma((n,)),
            dma((n,)), dma((n,)),
        ],
        compiler_params=pltpu.CompilerParams(
            collective_id=0, has_side_effects=True, vmem_limit_bytes=56 * 1024 * 1024
        ),
        name="step",
    )(flat, w_in, w_out, probe_vectors, key_queue, target_position.reshape(1, own))

    slots_total = slots * n
    start = lax.rem(pointer - lax.axis_index("mem") * slots + slots_total, slots_total)
    count = sessions * n
    start = jnp.where(start > slots_total - count, start - slots_total, start)
    block = min(512, slots)
    loss, grad, new_memory = pl.pallas_call(
        functools.partial(fill_kernel, block),
        out_shape=(
            jax.ShapeDtypeStruct((1, own), f32),
            jax.ShapeDtypeStruct((own, width), f32),
            jax.ShapeDtypeStruct(key_queue.shape, bf16),
        ),
        in_specs=[pl.BlockSpec(memory_space=pltpu.SMEM), HBM, VMEM, VMEM, VMEM],
        out_specs=(VMEM, VMEM, HBM),
        scratch_shapes=[
            pltpu.VMEM((count, width), bf16),
            pltpu.VMEM((count + 2 * block + 16, width), bf16),
            pltpu.VMEM(key_queue.shape, bf16),
            dma,
            dma((slots // block,)),
        ],
        compiler_params=pltpu.CompilerParams(vmem_limit_bytes=61000 * 1024),
        name="fill",
    )(start, keys, key_queue, loss, grad)
    return (loss.reshape(own), grad, new_memory)


def solution(mesh):
    placed = (
        P("mem", None, None),
        P(None, "feat"),
        P("feat", None),
        P(("mem", "feat"), None),
        P("mem", None),
        P(("mem", "feat")),
        P(),
    )
    return jax.shard_map(
        shards,
        mesh=mesh,
        in_specs=placed,
        out_specs=(P(("mem", "feat")), P(("mem", "feat"), None), P("mem", None)),
        check_vma=False,
    )
```

profile of v0, /device:TPU:0, one launch (start us, length us, event | category | flops | bytes accessed | tf_op | source)
XLA Modules:
  0.0 44.8 jit_solution(12491140281449311077)
XLA Ops:
  1.3 38.5 %step.1 = (f32[1,64]{1,0:T(1,128)}, f32[64,256]{1,0:T(8,128)}, bf16[2048,256]{1,0:T(8,128)(2,1)}) custom-call(bf16[8192,256]{1,0:T(8,128)(2,1)} %bitcast.4, bf16[256,256]{1,0:T(8,128)(2,1)} %w_in_ref.1, bf16[256,256]{1,0:T(8,128)(2,1)} %w_out_ref.1, bf16[64,256]{1,0:T(8,128)(2,1)} %probe_ref.1, bf16[8192,256]{1,0:T(8,128)(2,1)} %queue_ref.1, s32[1,64]{1,0:T(1,128)} %bitcast.5), custom_call_target="tpu_custom_call" | custom-call | tf_op jit(solution)/shard_map/step/pallas_call | solution.py:380
  39.8 5.0 %fill.1 = (f32[1,64]{1,0:T(1,128)}, f32[64,256]{1,0:T(8,128)}, bf16[8192,256]{1,0:T(8,128)(2,1)}) custom-call(s32[1]{0:T(128)S(6)} %select_n.4.start_ref, bf16[2048,256]{1,0:T(8,128)(2,1)} %get-tuple-element.9.keys_hbm, bf16[8192,256]{1,0:T(8,128)(2,1)} %queue_ref.1, f32[1,64]{1,0:T(1,128)} %get-tuple-element.10.loss_in, f32[64,256]{1,0:T(8,128)} %get-tuple-element.11.grad_in), custom_call_target="tpu_custom_call" | custom-call | tf_op jit(solution)/shard_map/fill/pallas_call | solution.py:429
where the time goes:
time: 45.1 us; the launch traced here: 44.8 us
  Pallas kernels  43.5 us (96%)
  between operations  1.3 us (3%)
    pallas_call x1, Pallas kernels, shards(): pl.pallas_call(functools.partial(step_kernel, n, nf, ev_chunk, slot_block...  38.5 us
    pallas_call x1, Pallas kernels, shards(): pl.pallas_call(functools.partial(fill_kernel, block), out_shape=(jax.Shap...  4.97 us

commit v1 on v0

v1 whole, which is shorter than its diff:
```python
import functools

import jax
import jax.numpy as jnp
from jax import lax
from jax.experimental import pallas as pl
from jax.experimental.pallas import tpu as pltpu
from jax.sharding import PartitionSpec as P

inverse_softness = 14.0
epsilon = 1e-06
log2e = 1.4426950408889634
MESH = pl.DeviceIdType.MESH
VMEM = pl.BlockSpec(memory_space=pltpu.VMEM)
HBM = pl.BlockSpec(memory_space=pltpu.HBM)
STEP_VMEM = 56 * 1024 * 1024
FILL_VMEM = 61000 * 1024


def flip(v, k):
    b = 1
    while b <= k:
        if k & b:
            v = v + b * (1 - 2 * lax.rem(lax.div(v, b), 2))
        b *= 2
    return v


def bits_of(n):
    out, b = [], 1
    while b < n:
        out.append(b)
        b *= 2
    return out[::-1]


def low_bit(s):
    return s & (-s)


def query_order(n):
    return list(range(n // 2, n)) + list(range(n // 2))


def step_kernel(
    n, nf, slot_block, q_chunk,
    ev_hbm, w_in_hbm, w_out_hbm, probe_hbm, queue_hbm, target_hbm,
    loss_ref, grad_ref, keys_ref,
    ev, w_in, w_out, queue, q_all, t_all, wide, partial, part_in, pos, m_s, l_s, acc,
    picked, h_in, stat_out, stat_in, gout, g_in, sims,
    ev_sem, in_sem, queue_sem, q_ss, q_rs, t_ss, t_rs, p_ss, p_rs, k_ss, k_rs,
    s_ss, s_rs, g_ss, g_rs, h_ss, h_rs,
):
    me = lax.axis_index("mem")
    mf = lax.axis_index("feat")
    slots, width = queue.shape
    own = q_all.shape[0] // n
    rows_q = n * own
    piece = ev.shape[1]
    n_blk = slots // slot_block
    part_rows = partial.shape[1]
    per_event = piece // part_rows
    order = query_order(n)
    place = {s: i for i, s in enumerate(order)}
    feats = list(range(nf - 1, -1, -1))
    f32, bf16 = jnp.float32, jnp.bfloat16

    def mem_peer(k):
        return (flip(me, k), mf)

    def feat_peer(k):
        return (me, flip(mf, k))

    def remote(src, dst, ss, rs, to):
        return pltpu.make_async_remote_copy(
            src_ref=src, dst_ref=dst, send_sem=ss, recv_sem=rs, device_id=to, device_id_type=MESH
        )

    barrier = pltpu.get_barrier_semaphore()
    for k in range(1, n):
        pl.semaphore_signal(barrier, inc=1, device_id=mem_peer(k), device_id_type=MESH)
    for k in range(1, nf):
        pl.semaphore_signal(barrier, inc=1, device_id=feat_peer(k), device_id_type=MESH)

    def rows_at(s):
        return pl.ds(place[s] * own, own)

    w_in_copy = pltpu.make_async_copy(w_in_hbm, w_in, in_sem.at[0])
    w_out_copy = pltpu.make_async_copy(w_out_hbm, w_out, in_sem.at[1])
    probe_copy = pltpu.make_async_copy(probe_hbm, q_all.at[rows_at(0)], in_sem.at[2])
    target_copy = pltpu.make_async_copy(target_hbm, t_all.at[0], in_sem.at[3])

    def ev_copy(i):
        at = pl.ds(pl.multiple_of(flip(mf, feats[i]) * piece, piece), piece)
        return pltpu.make_async_copy(ev_hbm.at[at], ev.at[i], ev_sem.at[i])

    def queue_copy(b):
        span = pl.ds(b * slot_block, slot_block)
        return pltpu.make_async_copy(queue_hbm.at[span], queue.at[span], queue_sem.at[b])

    w_in_copy.start()
    ev_copy(0).start()
    target_copy.start()
    w_out_copy.start()
    probe_copy.start()
    ahead = [ev_copy(i) for i in range(1, nf)] + [queue_copy(b) for b in range(n_blk)]

    def load_next(count):
        for a in ahead[:count]:
            a.start()
        del ahead[:count]

    load_next(1)

    pl.semaphore_wait(barrier, n - 1 + nf - 1)
    q_copies = {
        k: remote(probe_hbm, q_all.at[rows_at(k)], q_ss.at[k], q_rs.at[k], mem_peer(k))
        for k in range(n - 1, 0, -1)
    }
    t_copies = {
        k: remote(target_hbm, t_all.at[k], t_ss.at[k], t_rs.at[k], mem_peer(k))
        for k in range(n - 1, 0, -1)
    }
    for a in t_copies.values():
        a.start()
    for a in q_copies.values():
        a.start()

    c1 = 0.7978845608028654
    c2 = c1 * 0.044715

    def project(i):
        ev_copy(i).wait()
        load_next(len(ahead) if i == nf - 1 else 1)
        wide[i % 2] = jnp.dot(ev[i], w_in[...], preferred_element_type=f32)

    def encode(i):
        if i + 1 < nf:
            project(i + 1)
        x = wide[i % 2]
        y = x * jnp.tanh(x * (c1 + c2 * (x * x))) + x
        y = y.reshape(part_rows, per_event, y.shape[1])
        mean = jnp.sum(y, axis=1) * (0.5 / per_event)
        partial[feats[i]] = jnp.dot(mean.astype(bf16), w_out[...], preferred_element_type=f32)

    p_copies = []

    def send_partial(i):
        f = feats[i]
        if f:
            a = remote(partial.at[f], part_in.at[f], p_ss.at[f], p_rs.at[f], feat_peer(f))
            a.start()
            p_copies.append(a)

    w_in_copy.wait()
    project(0)
    w_out_copy.wait()
    for i in range(nf):
        encode(i)
        send_partial(i)
    probe_copy.wait()
    target_copy.wait()

    diag = lax.broadcasted_iota(jnp.int32, (own, own), 0) == lax.broadcasted_iota(
        jnp.int32, (own, own), 1
    )

    def as_column(row):
        wide_row = jnp.broadcast_to(row, (own, own))
        return jnp.sum(jnp.where(diag, wide_row, 0.0), axis=1, keepdims=True)

    chunk_blocks = q_chunk // own
    n_chunk = rows_q // q_chunk

    def slots_of(c):
        return order[c * chunk_blocks : (c + 1) * chunk_blocks]

    at = lax.broadcasted_iota(jnp.int32, (q_chunk, slot_block), 1)

    def pick(c):
        rs = slice(c * q_chunk, (c + 1) * q_chunk)
        for s in slots_of(c):
            if s:
                t_copies[s].wait_recv()
            local = as_column(t_all[s].astype(f32)).astype(jnp.int32) - me * slots
            pos[place[s] * own : (place[s] + 1) * own, :] = jnp.broadcast_to(local, (own, 128))
        for b in range(n_blk):
            if c == 0:
                queue_copy(b).wait()
            hit = at == (pos[rs, :1] - b * slot_block)
            v = jnp.dot(
                jnp.where(hit, 1.0, 0.0).astype(bf16),
                queue[b * slot_block : (b + 1) * slot_block, :],
                preferred_element_type=f32,
            )
            if b == 0:
                acc[rs, :] = v
            else:
                acc[rs, :] += v
        for s in slots_of(c):
            picked[s] = acc[rows_at(s), :].astype(bf16)

    h_copies = {}

    def h_send(bit):
        for s in range(n):
            if s and low_bit(s) == bit:
                h_copies[s] = remote(picked.at[s], h_in.at[s], h_ss.at[s], h_rs.at[s], mem_peer(bit))
                h_copies[s].start()

    def h_take(bit):
        for s in range(n):
            if s and low_bit(s) == bit:
                h_copies[s].wait_recv()
                picked[s ^ bit] = picked[s ^ bit] + h_in[s]

    for c in range(n_chunk):
        pick(c)
    h_send(1)

    k_copies = {}

    def key_span(r):
        m, f = flip(me, r[0]), flip(mf, r[1])
        return pl.ds(pl.multiple_of((m * nf + f) * part_rows, part_rows), part_rows)

    def onward(r):
        m, f = r
        out = []
        if r == (0, 0):
            out += [("m", k) for k in range(n - 2, 0, -2)]
        if f == 0 and m % 2 == 0:
            out.append(("m", 1))
        return out + [("f", b) for b in bits_of(nf) if not f or b < low_bit(f)]

    def pass_on(*r):
        if r != (0, 0):
            k_copies[r].wait_recv()
        span = key_span(r)
        for axis, b in onward(r):
            to = mem_peer(b) if axis == "m" else feat_peer(b)
            d = (r[0] ^ b, r[1]) if axis == "m" else (r[0], r[1] ^ b)
            j = d[0] * nf + d[1]
            k_copies[d] = remote(keys_ref.at[span], keys_ref.at[span], k_ss.at[j], k_rs.at[j], to)
            k_copies[d].start()

    def make_keys():
        for a in p_copies:
            a.wait_recv()
        raw = partial[0]
        for f in range(1, nf):
            raw = raw + part_in[f]
        scaled = raw * lax.rsqrt(jnp.mean(raw * raw, axis=1, keepdims=True) + epsilon) / 16.0
        keys_ref[key_span((0, 0)), :] = scaled.astype(bf16)
        pass_on(0, 0)

    make_keys()

    scale2 = inverse_softness * log2e
    work = [(c, b) for c in range(n_chunk) for b in range(n_blk)]
    q_seen = set()

    def similar(i):
        c, b = work[i]
        for s in slots_of(c):
            if s and s not in q_seen:
                q_seen.add(s)
                q_copies[s].wait_recv()
        sims[i % 2] = lax.dot_general(
            q_all[c * q_chunk : (c + 1) * q_chunk, :],
            queue[b * slot_block : (b + 1) * slot_block, :],
            (((1,), (1,)), ((), ())),
            preferred_element_type=f32,
        )

    def attend(i):
        c, b = work[i]
        rs = slice(c * q_chunk, (c + 1) * q_chunk)
        if i + 1 < len(work):
            similar(i + 1)
        s = sims[i % 2]
        m_new = jnp.broadcast_to(jnp.max(s, axis=1, keepdims=True), (q_chunk, 128))
        if b:
            m_old = m_s[rs, :]
            m_new = jnp.maximum(m_old, m_new)
            alpha = jnp.exp2((m_old - m_new) * scale2)
        m_s[rs, :] = m_new
        total, ps = None, []
        for j in range(slot_block // 128):
            p = jnp.exp2((s[:, j * 128 : (j + 1) * 128] - m_new) * scale2)
            total = p if total is None else total + p
            ps.append(p.astype(bf16))
        pv = jnp.dot(
            jnp.concatenate(ps, axis=1),
            queue[b * slot_block : (b + 1) * slot_block, :],
            preferred_element_type=f32,
        )
        if b:
            l_s[rs, :] = l_s[rs, :] * alpha + total
            for j in range(width // 128):
                cs = slice(j * 128, (j + 1) * 128)
                acc[rs, cs] = acc[rs, cs] * alpha + pv[:, cs]
        else:
            l_s[rs, :] = total
            acc[rs, :] = pv

    g_copies, s_copies = {}, {}

    def send_results(c):
        rs = slice(c * q_chunk, (c + 1) * q_chunk)
        for s in slots_of(c):
            if s:
                gout[s] = acc[rows_at(s), :].astype(bf16)
                g_copies[s] = remote(gout.at[s], g_in.at[s], g_ss.at[s], g_rs.at[s], mem_peer(s))
                g_copies[s].start()
        lane = lax.broadcasted_iota(jnp.int32, (q_chunk, 128), 1)
        sums = jnp.sum(l_s[rs, :], axis=1, keepdims=True)
        packed = jnp.where(lane == 0, m_s[rs, :], jnp.broadcast_to(sums, (q_chunk, 128))).T
        for i, s in enumerate(slots_of(c)):
            stat_out[s, 0:2, :] = packed[0:2, i * own : (i + 1) * own]
            if s:
                s_copies[s] = remote(stat_out.at[s], stat_in.at[s], s_ss.at[s], s_rs.at[s], mem_peer(s))
                s_copies[s].start()

    tasks = {}

    def later(frac, fn, *args):
        tasks.setdefault(int(frac * (len(work) - 1) + 0.5), []).append((fn, args))

    mem_bits = bits_of(n)[::-1]

    def step_h(j):
        h_take(mem_bits[j])
        if j + 1 < len(mem_bits):
            h_send(mem_bits[j + 1])

    for j in range(len(mem_bits) - 1):
        later((j + 1) / 2 if len(mem_bits) == 3 else (j + 1) / len(mem_bits), step_h, j)
    evens, odds = list(range(2, n, 2)), list(range(3, n, 2))
    for i, k in enumerate([1] + evens):
        later(3 / 7 + i / (7 * len(evens)), pass_on, k, 0)
    later(6 / 7, pass_on, 3, 0)

    similar(0)
    for i, (c, b) in enumerate(work):
        attend(i)
        if b == n_blk - 1:
            send_results(c)
        for fn, args in tasks.get(i, []):
            fn(*args)

    for k in odds[1:]:
        pass_on(k, 0)
    for b in bits_of(nf):
        for f in range(b, nf, b):
            if low_bit(f) == b and b > 1:
                for m in range(n):
                    pass_on(m, f)
    step_h(len(mem_bits) - 1)

    paired = picked[0].astype(f32)
    score = jnp.sum(q_all[rows_at(0), :].astype(f32) * paired, axis=1, keepdims=True)
    score = jnp.sum(
        jnp.where(diag, jnp.broadcast_to(score, (own, own)), 0.0), axis=0, keepdims=True
    )
    for k in range(1, n):
        s_copies[k].wait_recv()
    stats = [stat_out[0]] + [stat_in[k] for k in range(1, n)]
    top = stats[0][0:1, :]
    for st in stats[1:]:
        top = jnp.maximum(top, st[0:1, :])
    powers = [jnp.exp2((st[0:1, :] - top) * scale2) for st in stats]
    total = stats[0][1:2, :] * powers[0]
    for st, w in zip(stats[1:], powers[1:]):
        total = total + st[1:2, :] * w
    loss_ref[...] = (top - score) * inverse_softness + jnp.log(total)
    grad = acc[rows_at(0), :] * as_column(powers[0] / total)
    for k in [order[i] for i in range(n) if order[i]]:
        g_copies[k].wait_recv()
        grad = grad + g_in[k].astype(f32) * as_column(powers[k] / total)
    grad_ref[...] = inverse_softness * (grad - paired)

    for f in range(1, nf, 2):
        for m in range(n):
            pass_on(m, f)
    for group in (t_copies, q_copies, k_copies, h_copies, s_copies, g_copies):
        for a in group.values():
            a.wait_send()
    for a in p_copies:
        a.wait_send()


def fill_kernel(
    block, start_ref, keys_hbm, queue_ref, loss_in, grad_in,
    loss_ref, grad_ref, out_hbm,
    keys, rolled, merged, keys_sem, out_sem,
):
    start = start_ref[0]
    count = keys.shape[0]
    slots, width = queue_ref.shape
    phase = jnp.bitwise_and(start, 15)
    blocks = slots // block
    here = (start < slots) & (start + count > 0)
    keys_copy = pltpu.make_async_copy(keys_hbm, keys, keys_sem)

    @pl.when(here)
    def _():
        keys_copy.start()

    def spans(i):
        return slice(i * block, (i + 1) * block)

    def inside(i):
        return (i * block < start + count) & ((i + 1) * block > start)

    def plain(i):
        return pltpu.make_async_copy(queue_ref.at[spans(i)], out_hbm.at[spans(i)], out_sem.at[i])

    for i in range(blocks):

        @pl.when(jnp.logical_not(inside(i)))
        def _():
            plain(i).start()

    loss_ref[...] = loss_in[...]
    grad_ref[...] = grad_in[...]

    @pl.when(here)
    def _():
        keys_copy.wait()
        tile = min(256, count)
        for c in range(count // tile + 1):
            lo = max(c * tile - 16, 0)
            hi = min(c * tile + tile, count)
            x = keys[lo:hi, :].astype(jnp.float32)
            if c == 0:
                x = jnp.concatenate([jnp.zeros((16, width), jnp.float32), x], axis=0)
            if c == count // tile:
                x = jnp.concatenate([x, jnp.zeros((16, width), jnp.float32)], axis=0)
            x = pltpu.roll(x, phase, 0)[16:, :]
            at = block + c * tile
            rolled[at : at + x.shape[0], :] = x.astype(jnp.bfloat16)

    for i in range(blocks):

        @pl.when(inside(i))
        def _():
            at = pl.multiple_of(block + i * block - (start - phase), 16)
            row = lax.broadcasted_iota(jnp.int32, (block, width), 0) + (i * block - start)
            take = (row >= 0) & (row < count)
            new = rolled[pl.ds(at, block), :].astype(jnp.float32)
            old = queue_ref[spans(i), :].astype(jnp.float32)
            merged[spans(i), :] = jnp.where(take, new, old).astype(jnp.bfloat16)
            pltpu.make_async_copy(
                merged.at[spans(i)], out_hbm.at[spans(i)], out_sem.at[i]
            ).start()

    for i in range(blocks):
        plain(i).wait()


def shards(events, w_in, w_out, probe_vectors, key_queue, target_position, pointer):
    n, nf = lax.axis_size("mem"), lax.axis_size("feat")
    sessions, per, depth = events.shape
    own, width = probe_vectors.shape
    slots = key_queue.shape[0]
    rows_q = own * n
    hidden = w_in.shape[1]
    flat = events.reshape(sessions * per, depth)
    slot_block = min(2048, slots)
    q_chunk = min(256, rows_q)
    part_rows = sessions // nf
    piece = part_rows * per
    f32, bf16 = jnp.float32, jnp.bfloat16
    dma = pltpu.SemaphoreType.DMA
    loss, grad, keys = pl.pallas_call(
        functools.partial(step_kernel, n, nf, slot_block, q_chunk),
        out_shape=(
            jax.ShapeDtypeStruct((1, own), f32),
            jax.ShapeDtypeStruct((own, width), f32),
            jax.ShapeDtypeStruct((sessions * n, width), bf16),
        ),
        in_specs=[HBM] * 6,
        out_specs=(VMEM, VMEM, VMEM),
        scratch_shapes=[
            pltpu.VMEM((nf, piece, depth), bf16),
            pltpu.VMEM(w_in.shape, bf16),
            pltpu.VMEM(w_out.shape, bf16),
            pltpu.VMEM(key_queue.shape, bf16),
            pltpu.VMEM((rows_q, width), bf16),
            pltpu.VMEM((n, 1, own), jnp.int32),
            pltpu.VMEM((2, piece, hidden), f32),
            pltpu.VMEM((nf, part_rows, width), f32),
            pltpu.VMEM((nf, part_rows, width), f32),
            pltpu.VMEM((rows_q, 128), jnp.int32),
            pltpu.VMEM((rows_q, 128), f32),
            pltpu.VMEM((rows_q, 128), f32),
            pltpu.VMEM((rows_q, width), f32),
            pltpu.VMEM((n, own, width), bf16),
            pltpu.VMEM((n, own, width), bf16),
            pltpu.VMEM((n, 4, own), f32),
            pltpu.VMEM((n, 4, own), f32),
            pltpu.VMEM((n, own, width), bf16),
            pltpu.VMEM((n, own, width), bf16),
            pltpu.VMEM((2, q_chunk, slot_block), f32),
            dma((nf,)),
            dma((4,)),
            dma((slots // slot_block,)),
            dma((n,)), dma((n,)), dma((n,)), dma((n,)),
            dma((nf,)), dma((nf,)),
            dma((n * nf,)), dma((n * nf,)),
            dma((n,)), dma((n,)),
            dma((n,)), dma((n,)),
            dma((n,)), dma((n,)),
        ],
        compiler_params=pltpu.CompilerParams(
            collective_id=0, has_side_effects=True, vmem_limit_bytes=STEP_VMEM
        ),
        name="step",
    )(flat, w_in, w_out, probe_vectors, key_queue, target_position.reshape(1, own))

    slots_total = slots * n
    start = lax.rem(pointer - lax.axis_index("mem") * slots + slots_total, slots_total)
    count = sessions * n
    start = jnp.where(start > slots_total - count, start - slots_total, start)
    block = min(512, slots)
    loss, grad, new_memory = pl.pallas_call(
        functools.partial(fill_kernel, block),
        out_shape=(
            jax.ShapeDtypeStruct((1, own), f32),
            jax.ShapeDtypeStruct((own, width), f32),
            jax.ShapeDtypeStruct(key_queue.shape, bf16),
        ),
        in_specs=[pl.BlockSpec(memory_space=pltpu.SMEM), HBM, VMEM, VMEM, VMEM],
        out_specs=(VMEM, VMEM, HBM),
        scratch_shapes=[
            pltpu.VMEM((count, width), bf16),
            pltpu.VMEM((count + 2 * block + 16, width), bf16),
            pltpu.VMEM(key_queue.shape, bf16),
            dma,
            dma((slots // block,)),
        ],
        compiler_params=pltpu.CompilerParams(vmem_limit_bytes=FILL_VMEM),
        name="fill",
    )(start, keys, key_queue, loss, grad)
    return (loss.reshape(own), grad, new_memory)


def solution(mesh):
    placed = (
        P("mem", None, None),
        P(None, "feat"),
        P("feat", None),
        P(("mem", "feat"), None),
        P("mem", None),
        P(("mem", "feat")),
        P(),
    )
    return jax.shard_map(
        shards,
        mesh=mesh,
        in_specs=placed,
        out_specs=(P(("mem", "feat")), P(("mem", "feat"), None), P("mem", None)),
        check_vma=False,
    )
```

time: 45.1 us -> 41.2 us (0.914)
  Pallas kernels: 43.5 us -> 39.6 us
    pallas_call x1, Pallas kernels: 38.5 us -> 34.6 us  [shards(): pl.pallas_call(functools.partial(step_kernel, n, nf, slot_block, q_chunk)...]
where the time goes in v1:
time: 41.2 us; the launch traced here: 41.1 us
  Pallas kernels  39.6 us (96%)
  between operations  1.46 us (4%)
    pallas_call x1, Pallas kernels, shards(): pl.pallas_call(functools.partial(step_kernel, n, nf, slot_block, q_chunk)...  34.6 us
    pallas_call x1, Pallas kernels, shards(): pl.pallas_call(functools.partial(fill_kernel, block), out_shape=(jax.Shap...  4.97 us

profile of v1, /device:TPU:0, one launch (start us, length us, event | category | flops | bytes accessed | tf_op | source)
XLA Modules:
  0.0 41.1 jit_solution(3481901996966735823)
XLA Ops:
  1.3 34.6 %step.1 = (f32[1,64]{1,0:T(1,128)}, f32[64,256]{1,0:T(8,128)}, bf16[2048,256]{1,0:T(8,128)(2,1)}) custom-call(bf16[8192,256]{1,0:T(8,128)(2,1)} %bitcast.4, bf16[256,256]{1,0:T(8,128)(2,1)} %w_in_hbm.1, bf16[256,256]{1,0:T(8,128)(2,1)} %w_out_hbm.1, bf16[64,256]{1,0:T(8,128)(2,1)} %probe_hbm.1, bf16[8192,256]{1,0:T(8,128)(2,1)} %queue_ref.1, s32[1,64]{1,0:T(1,128)} %bitcast.5), custom_call_target="tpu_custom_call" | custom-call | tf_op jit(solution)/shard_map/step/pallas_call | solution.py:476
  36.0 5.0 %fill.1 = (f32[1,64]{1,0:T(1,128)}, f32[64,256]{1,0:T(8,128)}, bf16[8192,256]{1,0:T(8,128)(2,1)}) custom-call(s32[1]{0:T(128)S(6)} %select_n.4.start_ref, bf16[2048,256]{1,0:T(8,128)(2,1)} %get-tuple-element.9.keys_hbm, bf16[8192,256]{1,0:T(8,128)(2,1)} %queue_ref.1, f32[1,64]{1,0:T(1,128)} %get-tuple-element.10.loss_in, f32[64,256]{1,0:T(8,128)} %get-tuple-element.11.grad_in), custom_call_target="tpu_custom_call" | custom-call | tf_op jit(solution)/shard_map/fill/pallas_call | solution.py:527

commit v2 on v1

--- a/solution.py
+++ b/solution.py
@@ -13,8 +13,8 @@
 MESH = pl.DeviceIdType.MESH
 VMEM = pl.BlockSpec(memory_space=pltpu.VMEM)
 HBM = pl.BlockSpec(memory_space=pltpu.HBM)
-STEP_VMEM = 56 * 1024 * 1024
-FILL_VMEM = 61000 * 1024
+STEP_VMEM = 40 * 1024 * 1024
+FILL_VMEM = 24 * 1024 * 1024
 
 
 def flip(v, k):
@@ -103,14 +103,10 @@
     target_copy.start()
     w_out_copy.start()
     probe_copy.start()
-    ahead = [ev_copy(i) for i in range(1, nf)] + [queue_copy(b) for b in range(n_blk)]
-
-    def load_next(count):
-        for a in ahead[:count]:
-            a.start()
-        del ahead[:count]
-
-    load_next(1)
+    for i in range(1, nf):
+        ev_copy(i).start()
+    for b in range(n_blk):
+        queue_copy(b).start()
 
     pl.semaphore_wait(barrier, n - 1 + nf - 1)
     q_copies = {
@@ -130,8 +126,6 @@
     c2 = c1 * 0.044715
 
     def project(i):
-        ev_copy(i).wait()
-        load_next(len(ahead) if i == nf - 1 else 1)
         wide[i % 2] = jnp.dot(ev[i], w_in[...], preferred_element_type=f32)
 
     def encode(i):
@@ -153,13 +147,22 @@
             p_copies.append(a)
 
     w_in_copy.wait()
+    ev_copy(0).wait()
     project(0)
     w_out_copy.wait()
-    for i in range(nf):
-        encode(i)
-        send_partial(i)
     probe_copy.wait()
     target_copy.wait()
+    for i in range(1, nf):
+        ev_copy(i).wait()
+    half = nf // 2
+    for i in range(half):
+        encode(i)
+    for i in range(half):
+        send_partial(i)
+    for i in range(half, nf):
+        encode(i)
+    for i in range(half, nf):
+        send_partial(i)
 
     diag = lax.broadcasted_iota(jnp.int32, (own, own), 0) == lax.broadcasted_iota(
         jnp.int32, (own, own), 1
@@ -180,13 +183,9 @@
     def pick(c):
         rs = slice(c * q_chunk, (c + 1) * q_chunk)
         for s in slots_of(c):
-            if s:
-                t_copies[s].wait_recv()
             local = as_column(t_all[s].astype(f32)).astype(jnp.int32) - me * slots
             pos[place[s] * own : (place[s] + 1) * own, :] = jnp.broadcast_to(local, (own, 128))
         for b in range(n_blk):
-            if c == 0:
-                queue_copy(b).wait()
             hit = at == (pos[rs, :1] - b * slot_block)
             v = jnp.dot(
                 jnp.where(hit, 1.0, 0.0).astype(bf16),
@@ -214,6 +213,10 @@
                 h_copies[s].wait_recv()
                 picked[s ^ bit] = picked[s ^ bit] + h_in[s]
 
+    for k in range(1, n):
+        t_copies[k].wait_recv()
+    for b in range(n_blk):
+        queue_copy(b).wait()
     for c in range(n_chunk):
         pick(c)
     h_send(1)
@@ -334,12 +337,13 @@
         if j + 1 < len(mem_bits):
             h_send(mem_bits[j + 1])
 
-    for j in range(len(mem_bits) - 1):
-        later((j + 1) / 2 if len(mem_bits) == 3 else (j + 1) / len(mem_bits), step_h, j)
     evens, odds = list(range(2, n, 2)), list(range(3, n, 2))
-    for i, k in enumerate([1] + evens):
-        later(3 / 7 + i / (7 * len(evens)), pass_on, k, 0)
-    later(6 / 7, pass_on, 3, 0)
+    for k in [1, 2]:
+        later(3 / 7, pass_on, k, 0)
+    for k in evens[1:]:
+        later(5 / 7, pass_on, k, 0)
+    later(5 / 7, step_h, 0)
+    later(1, pass_on, 3, 0)
 
     similar(0)
     for i, (c, b) in enumerate(work):
@@ -351,12 +355,14 @@
 
     for k in odds[1:]:
         pass_on(k, 0)
+    step_h(1)
     for b in bits_of(nf):
         for f in range(b, nf, b):
             if low_bit(f) == b and b > 1:
                 for m in range(n):
                     pass_on(m, f)
-    step_h(len(mem_bits) - 1)
+    for j in range(2, len(mem_bits)):
+        step_h(j)
 
     paired = picked[0].astype(f32)
     score = jnp.sum(q_all[rows_at(0), :].astype(f32) * paired, axis=1, keepdims=True)
@@ -517,7 +523,12 @@
             collective_id=0, has_side_effects=True, vmem_limit_bytes=STEP_VMEM
         ),
         name="step",
-    )(flat, w_in, w_out, probe_vectors, key_queue, target_position.reshape(1, own))
+    )(
+        *(
+            pltpu.with_memory_space_constraint(a, pltpu.HBM)
+            for a in (flat, w_in, w_out, probe_vectors, key_queue, target_position.reshape(1, own))
+        )
+    )
 
     slots_total = slots * n
     start = lax.rem(pointer - lax.axis_index("mem") * slots + slots_total, slots_total)

time: 41.2 us -> 33.8 us (0.82)
  Pallas kernels: 39.6 us -> 32.2 us
    pallas_call x1, Pallas kernels: 34.6 us -> 29.3 us  [shards(): pl.pallas_call(functools.partial(step_kernel, n, nf, slot_block, q_chunk)...]
    pallas_call x1, Pallas kernels: 4.97 us -> 2.93 us  [shards(): pl.pallas_call(functools.partial(fill_kernel, block), out_shape=(jax.Shap...]
where the time goes in v2:
time: 33.8 us; the launch traced here: 33.7 us
  Pallas kernels  32.2 us (95%)
  between operations  1.48 us (4%)
    pallas_call x1, Pallas kernels, shards(): pl.pallas_call(functools.partial(step_kernel, n, nf, slot_block, q_chunk)...  29.3 us
    pallas_call x1, Pallas kernels, shards(): pl.pallas_call(functools.partial(fill_kernel, block), out_shape=(jax.Shap...  2.93 us

profile of v2, /device:TPU:0, one launch (start us, length us, event | category | flops | bytes accessed | tf_op | source)
XLA Modules:
  0.0 33.7 jit_solution(13300281426014192697)
XLA Ops:
  1.3 0.0 copy-start
  1.3 29.3 %step.1 = (f32[1,64]{1,0:T(1,128)S(1)}, f32[64,256]{1,0:T(8,128)S(1)}, bf16[2048,256]{1,0:T(8,128)(2,1)S(1)}) custom-call(bf16[8192,256]{1,0:T(8,128)(2,1)} %bitcast.4, bf16[256,256]{1,0:T(8,128)(2,1)} %w_in_hbm.1, bf16[256,256]{1,0:T(8,128)(2,1)} %w_out_hbm.1, bf16[64,256]{1,0:T(8,128)(2,1)} %probe_hbm.1, bf16[8192,256]{1,0:T(8,128)(2,1)} %queue_ref.1, ...), custom_call_target="tpu_custom_call" | custom-call | tf_op jit(solution)/shard_map/step/pallas_call | solution.py:482
  30.6 0.0 copy-done
  30.6 2.9 %fill.1 = (f32[1,64]{1,0:T(1,128)}, f32[64,256]{1,0:T(8,128)}, bf16[8192,256]{1,0:T(8,128)(2,1)}) custom-call(s32[1]{0:T(128)S(6)} %select_n.4.start_ref, bf16[2048,256]{1,0:T(8,128)(2,1)S(1)} %get-tuple-element.9.keys_hbm, bf16[8192,256]{1,0:T(8,128)(2,1)S(1)} %copy-done, f32[1,64]{1,0:T(1,128)S(1)} %get-tuple-element.10.loss_in, ...), custom_call_target="tpu_custom_call" | custom-call | tf_op jit(solution)/shard_map/fill/pallas_call | solution.py:538
Async XLA Ops:
  1.3 29.3 %copy-start = (bf16[8192,256]{1,0:T(8,128)(2,1)S(1)}, bf16[8192,256]{1,0:T(8,128)(2,1)}, u32[]{:S(2)}) copy-start(bf16[8192,256]{1,0:T(8,128)(2,1)} %queue_ref.1) | copy-start | bytes 12582916

commit v3 on v2

--- a/solution.py
+++ b/solution.py
@@ -45,8 +45,8 @@
 def step_kernel(
     n, nf, slot_block, q_chunk,
     ev_hbm, w_in_hbm, w_out_hbm, probe_hbm, queue_hbm, target_hbm,
-    loss_ref, grad_ref, keys_ref,
-    ev, w_in, w_out, queue, q_all, t_all, wide, partial, part_in, pos, m_s, l_s, acc,
+    loss_ref, grad_ref, keys_ref, queue,
+    ev, w_in, w_out, q_all, t_all, wide, partial, part_in, pos, m_s, l_s, acc,
     picked, h_in, stat_out, stat_in, gout, g_in, sims,
     ev_sem, in_sem, queue_sem, q_ss, q_rs, t_ss, t_rs, p_ss, p_rs, k_ss, k_rs,
     s_ss, s_rs, g_ss, g_rs, h_ss, h_rs,
@@ -81,6 +81,9 @@
         pl.semaphore_signal(barrier, inc=1, device_id=mem_peer(k), device_id_type=MESH)
     for k in range(1, nf):
         pl.semaphore_signal(barrier, inc=1, device_id=feat_peer(k), device_id_type=MESH)
+    across = nf // 2
+    diagonal = (flip(me, 1), flip(mf, across))
+    pl.semaphore_signal(barrier, inc=1, device_id=diagonal, device_id_type=MESH)
 
     def rows_at(s):
         return pl.ds(place[s] * own, own)
@@ -108,7 +111,7 @@
     for b in range(n_blk):
         queue_copy(b).start()
 
-    pl.semaphore_wait(barrier, n - 1 + nf - 1)
+    pl.semaphore_wait(barrier, n - 1 + nf - 1 + 1)
     q_copies = {
         k: remote(probe_hbm, q_all.at[rows_at(k)], q_ss.at[k], q_rs.at[k], mem_peer(k))
         for k in range(n - 1, 0, -1)
@@ -231,18 +234,18 @@
         m, f = r
         out = []
         if r == (0, 0):
-            out += [("m", k) for k in range(n - 2, 0, -2)]
+            out += [(k, 0) for k in range(n - 2, 0, -2)]
         if f == 0 and m % 2 == 0:
-            out.append(("m", 1))
-        return out + [("f", b) for b in bits_of(nf) if not f or b < low_bit(f)]
+            out += [(1, 0), (0, across), (1, across)]
+        return out + [(0, b) for b in bits_of(across) if not f or b < low_bit(f)]
 
     def pass_on(*r):
         if r != (0, 0):
             k_copies[r].wait_recv()
         span = key_span(r)
-        for axis, b in onward(r):
-            to = mem_peer(b) if axis == "m" else feat_peer(b)
-            d = (r[0] ^ b, r[1]) if axis == "m" else (r[0], r[1] ^ b)
+        for dm, df in onward(r):
+            to = (flip(me, dm), flip(mf, df))
+            d = (r[0] ^ dm, r[1] ^ df)
             j = d[0] * nf + d[1]
             k_copies[d] = remote(keys_ref.at[span], keys_ref.at[span], k_ss.at[j], k_rs.at[j], to)
             k_copies[d].start()
@@ -338,12 +341,10 @@
             h_send(mem_bits[j + 1])
 
     evens, odds = list(range(2, n, 2)), list(range(3, n, 2))
-    for k in [1, 2]:
-        later(3 / 7, pass_on, k, 0)
+    later(3 / 7, pass_on, 2, 0)
     for k in evens[1:]:
         later(5 / 7, pass_on, k, 0)
     later(5 / 7, step_h, 0)
-    later(1, pass_on, 3, 0)
 
     similar(0)
     for i, (c, b) in enumerate(work):
@@ -353,14 +354,18 @@
         for fn, args in tasks.get(i, []):
             fn(*args)
 
-    for k in odds[1:]:
-        pass_on(k, 0)
     step_h(1)
-    for b in bits_of(nf):
-        for f in range(b, nf, b):
-            if low_bit(f) == b and b > 1:
-                for m in range(n):
-                    pass_on(m, f)
+    pass_on(1, 0)
+    for m in range(0, n, 2):
+        pass_on(m, across)
+    for m in range(3, n, 2):
+        pass_on(m, 0)
+    for m in range(1, n, 2):
+        pass_on(m, across)
+    for f in range(1, nf):
+        if f != across and low_bit(f) > 1:
+            for m in range(n):
+                pass_on(m, f)
     for j in range(2, len(mem_bits)):
         step_h(j)
 
@@ -479,20 +484,20 @@
     piece = part_rows * per
     f32, bf16 = jnp.float32, jnp.bfloat16
     dma = pltpu.SemaphoreType.DMA
-    loss, grad, keys = pl.pallas_call(
+    loss, grad, keys, held = pl.pallas_call(
         functools.partial(step_kernel, n, nf, slot_block, q_chunk),
         out_shape=(
             jax.ShapeDtypeStruct((1, own), f32),
             jax.ShapeDtypeStruct((own, width), f32),
             jax.ShapeDtypeStruct((sessions * n, width), bf16),
+            jax.ShapeDtypeStruct(key_queue.shape, bf16),
         ),
         in_specs=[HBM] * 6,
-        out_specs=(VMEM, VMEM, VMEM),
+        out_specs=(VMEM, VMEM, VMEM, VMEM),
         scratch_shapes=[
             pltpu.VMEM((nf, piece, depth), bf16),
             pltpu.VMEM(w_in.shape, bf16),
             pltpu.VMEM(w_out.shape, bf16),
-            pltpu.VMEM(key_queue.shape, bf16),
             pltpu.VMEM((rows_q, width), bf16),
             pltpu.VMEM((n, 1, own), jnp.int32),
             pltpu.VMEM((2, piece, hidden), f32),
@@ -553,7 +558,7 @@
         ],
         compiler_params=pltpu.CompilerParams(vmem_limit_bytes=FILL_VMEM),
         name="fill",
-    )(start, keys, key_queue, loss, grad)
+    )(start, keys, held, loss, grad)
     return (loss.reshape(own), grad, new_memory)
 
 

time: 33.8 us -> 33.7 us (level)
  no operation moved by 1% of the time
where the time goes in v3:
time: 33.7 us; the launch traced here: 33.5 us
  Pallas kernels  32.1 us (95%)
  between operations  1.46 us (4%)
    pallas_call x1, Pallas kernels, shards(): pl.pallas_call(functools.partial(step_kernel, n, nf, slot_block, q_chunk)...  29.3 us
    pallas_call x1, Pallas kernels, shards(): pl.pallas_call(functools.partial(fill_kernel, block), out_shape=(jax.Shap...  2.79 us

profile of v3, /device:TPU:0, one launch (start us, length us, event | category | flops | bytes accessed | tf_op | source)
XLA Modules:
  0.0 33.5 jit_solution(8497273372870012301)
XLA Ops:
  1.3 29.3 %step.1 = (f32[1,64]{1,0:T(1,128)S(1)}, f32[64,256]{1,0:T(8,128)S(1)}, bf16[2048,256]{1,0:T(8,128)(2,1)S(1)}, bf16[8192,256]{1,0:T(8,128)(2,1)S(1)}) custom-call(bf16[8192,256]{1,0:T(8,128)(2,1)} %bitcast.4, bf16[256,256]{1,0:T(8,128)(2,1)} %w_in_hbm.1, bf16[256,256]{1,0:T(8,128)(2,1)} %w_out_hbm.1, bf16[64,256]{1,0:T(8,128)(2,1)} %probe_hbm.1, ...), custom_call_target="tpu_custom_call" | custom-call | tf_op jit(solution)/shard_map/step/pallas_call | solution.py:487
  30.6 2.8 %fill.1 = (f32[1,64]{1,0:T(1,128)}, f32[64,256]{1,0:T(8,128)}, bf16[8192,256]{1,0:T(8,128)(2,1)}) custom-call(s32[1]{0:T(128)S(6)} %select_n.4.start_ref, bf16[2048,256]{1,0:T(8,128)(2,1)S(1)} %get-tuple-element.10.keys_hbm, bf16[8192,256]{1,0:T(8,128)(2,1)S(1)} %get-tuple-element.11.queue_ref, f32[1,64]{1,0:T(1,128)S(1)} %get-tuple-element.12.loss_in, ...), custom_call_target="tpu_custom_call" | custom-call | tf_op jit(solution)/shard_map/fill/pallas_call | solution.py:543
